TPU v7x, 32 devices: a whole 2x2x4 slice. The times are simulated.
32 devices in a mesh: seq: 4 (over z), phase: 4 (over y, x), dp: 2 (over core).
Axes of the slice: x: 2, y: 2, z: 4, core: 2. Of those that a mesh axis runs over, the one named last changes fastest.
Arguments:
- byte_embed: bfloat16 [4096, 1536], P(('dp', 'seq')), parts along dimension 0, may hold values from -6 to 6
- in_gain: float32 [1536], replicated, may hold values from 0.25 to 1.75
- w_qkv: bfloat16 [1536, 3, 1536], P('seq', None, 'phase')
- w_up: bfloat16 [1536, 3072], P('phase')
- out_gain: float32 [3072], P('phase'), may hold values from 0.25 to 1.75
- bounds: int32 [1024], P(('dp', 'seq')), parts along dimension 0, may hold values from 0 to 2047, as said below
- owner: int32 [1024, 1], P(('dp', 'seq')), parts along dimension 0, may hold values from 0 to 3; in each aligned block of 128 rows (0 to 127, 128 to 255, ...) at most 64 rows name the same one
Outputs:
- byte_states: bfloat16 [4096, 1536], P(('dp', 'seq'), 'phase'), parts along dimension 0
- stretch_states: bfloat16 [2048, 3072], P(('dp', 'seq'), 'phase'), parts along dimension 0
There are 2 independent parts, one for each index of `dp`. A program takes and returns all parts, laid end to end along the dimension named above; an argument that names none is the same for every part. Nothing has to cross between parts.
Inputs may be any that keep to these rules, and one draw needn't show every extreme that they name: `bounds`: strictly rising; the 128 entries of block b lie in bytes b * 512 to (b + 1) * 512 - 1, and the first and last byte of each block are among them. Among the 128 stretch rows of one block no owner is named more than 64 times.
All inputs are finite; a program needn't handle non-finite values.
Results may differ from a plain program's by a relative error of at most 0.013.
Values may be sent and summed in bfloat16 or wider, within the bound.
A program may use at most 128 MiB of HBM per device.

v0:
```python
import jax
import jax.numpy as jnp
from jax import lax
from jax.sharding import PartitionSpec as P

DC = 3072
HD = 128
WINDOW = 1024


def passed_along(value, axis, by):
    devices = lax.axis_size(axis)
    pairs = [(i, i + by) for i in range(devices) if 0 <= i + by < devices]
    return lax.ppermute(value, axis, pairs)


def project_rows(rows, w_up, out_gain):
    groups = lax.axis_size("phase")
    full_rows = lax.all_gather(rows, "phase", axis=1, tiled=True)
    w_cols = lax.all_to_all(w_up, "phase", split_axis=1, concat_axis=0, tiled=True)
    count = full_rows.shape[0]
    width = rows.shape[1]
    columns = w_cols.shape[1]
    pieces = jnp.einsum(
        "nsg,sgc->snc",
        full_rows.reshape(count, groups, width),
        w_cols.reshape(groups, width, columns),
        preferred_element_type=jnp.float32,
    )
    projected = jnp.sum(pieces.astype(jnp.bfloat16).astype(jnp.float32), axis=0)
    squares = lax.psum(jnp.sum(projected * projected, axis=1), "phase")
    scale = lax.rsqrt(squares / DC + 1e-05)
    return (projected * scale[:, None] * out_gain).astype(jnp.bfloat16)


def on_device(byte_embed, in_gain, w_qkv, w_up, out_gain, bounds, owner):
    tok = byte_embed.shape[0]
    n_seq = lax.axis_size("seq")
    mine = lax.axis_index("seq")
    section = lax.axis_index("phase")
    width_dev = w_qkv.shape[2]
    heads_dev = width_dev // HD
    x32 = byte_embed.astype(jnp.float32)
    normed = (x32 * lax.rsqrt(jnp.mean(x32 * x32, axis=1, keepdims=True) + 1e-05) * in_gain).astype(
        jnp.bfloat16
    )
    piece = lax.all_gather(w_qkv, "seq", axis=0, tiled=True)
    qkv = jnp.dot(
        normed, piece.reshape(piece.shape[0], 3 * width_dev), preferred_element_type=jnp.float32
    ).astype(jnp.bfloat16)
    qkv = qkv.reshape(tok, 3, heads_dev, HD)
    query = qkv[:, 0]
    keys = qkv[:, 1]
    values = qkv[:, 2]
    reach = -(-WINDOW // tok)
    key_list = [keys]
    value_list = [values]
    for distance in range(1, reach + 1):
        earlier_keys, earlier_values = passed_along((keys, values), "seq", distance)
        key_list = [earlier_keys] + key_list
        value_list = [earlier_values] + value_list
    key_all = jnp.concatenate(key_list, axis=0)
    value_all = jnp.concatenate(value_list, axis=0)
    scores = jnp.einsum(
        "ihd,jhd->hij", query, key_all, preferred_element_type=jnp.float32
    ) * HD ** (-0.5)
    q_pos = mine * tok + jnp.arange(tok, dtype=jnp.int32)
    k_pos = mine * tok - reach * tok + jnp.arange((reach + 1) * tok, dtype=jnp.int32)
    keep = (
        (k_pos[None, :] <= q_pos[:, None])
        & (k_pos[None, :] > q_pos[:, None] - WINDOW)
        & (k_pos[None, :] >= 0)
    )
    scores = jnp.where(keep[None], scores, -jnp.inf)
    top = jnp.max(scores, axis=2, keepdims=True)
    expo = jnp.exp(scores - top)
    probs = (expo / jnp.sum(expo, axis=2, keepdims=True)).astype(jnp.bfloat16)
    attended = jnp.einsum(
        "hij,jhd->ihd", probs, value_all, preferred_element_type=jnp.float32
    ).astype(jnp.bfloat16)
    attended = attended.reshape(tok, width_dev)
    residual = lax.dynamic_slice_in_dim(x32, section * width_dev, width_dev, 1)
    byte_states = (residual + attended.astype(jnp.float32)).astype(jnp.bfloat16)
    local = bounds - mine * tok
    stretch_rows = jnp.take(byte_states, local, axis=0)
    owners = owner[:, 0]
    crows = owners.shape[0]
    slot_count = 2 * crows // n_seq
    place = jnp.arange(crows, dtype=jnp.int32)
    earlier = (owners[:, None] == owners[None, :]) & (place[None, :] < place[:, None])
    rank = jnp.sum(earlier.astype(jnp.int32), axis=1)
    target = owners * slot_count + rank
    placing = (target[None, :] == jnp.arange(n_seq * slot_count, dtype=jnp.int32)[:, None]).astype(
        jnp.bfloat16
    )
    outgoing = jnp.dot(placing, stretch_rows, preferred_element_type=jnp.float32).astype(
        jnp.bfloat16
    )
    outgoing = outgoing.reshape(n_seq, slot_count, width_dev)
    arrived = lax.all_to_all(outgoing, "seq", split_axis=0, concat_axis=0, tiled=True).reshape(
        n_seq * slot_count, width_dev
    )
    stretch_states = project_rows(arrived, w_up, out_gain)
    return (byte_states, stretch_states)


def solution(mesh):
    return jax.shard_map(
        on_device,
        mesh=mesh,
        in_specs=(
            P(("dp", "seq"), None),
            P(),
            P("seq", None, "phase"),
            P("phase", None),
            P("phase"),
            P(("dp", "seq")),
            P(("dp", "seq"), None),
        ),
        out_specs=(P(("dp", "seq"), "phase"), P(("dp", "seq"), "phase")),
        check_vma=False,
    )
```

profile of v0, /device:TPU:0, one launch (start us, length us, event | category | flops | bytes accessed | tf_op | source)
XLA Modules:
  0.0 220.7 jit_solution(122934458647829781)
XLA Ops:
  7.2 2.4 %copy.31 = bf16[384,3,384]{0,2,1:T(8,128)(2,1)} copy(bf16[384,3,384]{2,0,1:T(8,128)(2,1)} %param.9) | data formatting | bytes 1769472 | tf_op args[2]
  9.7 2.0 convert_element_type.44
  12.0 0.4 multiply_reduce_fusion
  12.4 69.8 %all-gather.2.cloned.1.call-done = bf16[1536,3,384]{0,2,1:T(8,128)(2,1)} async-done(((bf16[384,3,384]{0,2,1:T(8,128)(2,1)}), bf16[1536,3,384]{0,2,1:T(8,128)(2,1)}) %all-gather.2.cloned.1.call-update) | async-done | bytes 3538960 | tf_op jit(solution)/shard_map/all_gather | solution.py:47
  82.2 4.3 %convolution_convert_fusion = bf16[512,1152]{1,0:T(8,128)(2,1)S(1)} fusion(bf16[1536,1152]{0,1:T(8,128)(2,1)} %bitcast.36, f32[1536]{0:T(1024)S(1)} %copy-done.5, f32[512]{0:T(512)S(1)} %add_rsqrt_fusion, bf16[512,1536]{1,0:T(8,128)(2,1)S(1)} %copy-done), kind=kOutput, calls=%fused_computation.14 | convolution fusion | flops 1815674880 | bytes 6299648 | tf_op jit(solution)/shard_map/dot_general | solution.py:48
  86.5 0.6 copy.32
  87.1 0.9 slice_bitcast_fusion.2
  88.2 2.9 %collective-permute-start.2 = (bf16[512,3,128]{2,0,1:T(8,128)(2,1)S(1)}, bf16[512,3,128]{2,0,1:T(8,128)(2,1)S(1)}, u32[]{:S(2)}, u32[]{:S(2)}) collective-permute-start(bf16[512,3,128]{2,0,1:T(8,128)(2,1)S(1)} %bitcast.30), channel_id=1, source_target_pairs={{0,16},{8,24},{1,17},{9,25},{2,18},{10,26},{3,19},{11,27},{4,20},{... | collective-permute-start | bytes 1179656 | tf_op jit(solution)/shard_map/ppermute | solution.py:14
  91.1 2.4 %collective-permute-start.3 = (bf16[512,3,128]{2,0,1:T(8,128)(2,1)S(1)}, bf16[512,3,128]{2,0,1:T(8,128)(2,1)S(1)}, u32[]{:S(2)}, u32[]{:S(2)}) collective-permute-start(bf16[512,3,128]{2,0,1:T(8,128)(2,1)S(1)} %bitcast.31), channel_id=1, source_target_pairs={{0,8},{8,16},{16,24},{1,9},{9,17},{17,25},{2,10},{10,18},{18,26},{... | collective-permute-start | bytes 1179656 | tf_op jit(solution)/shard_map/ppermute | solution.py:14
  93.6 1.7 and_and_fusion
  95.3 2.0 collective-permute-start
  97.3 2.7 %collective-permute-start.1 = (bf16[512,3,128]{0,2,1:T(8,128)(2,1)}, bf16[512,3,128]{0,2,1:T(8,128)(2,1)}, u32[]{:S(2)}, u32[]{:S(2)}) collective-permute-start(bf16[512,3,128]{0,2,1:T(8,128)(2,1)} %get-tuple-element.4), channel_id=1, source_target_pairs={{0,8},{8,16},{16,24},{1,9},{9,17},{17,25},{2,10},{10,18},{18,26},{... | collective-permute-start | bytes 1179656 | tf_op jit(solution)/shard_map/ppermute | solution.py:14
  99.9 0.6 collective-permute-done.2
  100.6 8.4 %collective-permute-done.3 = bf16[512,3,128]{2,0,1:T(8,128)(2,1)S(1)} collective-permute-done((bf16[512,3,128]{2,0,1:T(8,128)(2,1)S(1)}, bf16[512,3,128]{2,0,1:T(8,128)(2,1)S(1)}, u32[]{:S(2)}, u32[]{:S(2)}) %collective-permute-start.3) | collective-permute-done | bytes 393248 | tf_op jit(solution)/shard_map/ppermute | solution.py:14
  109.0 2.4 %fusion.21 = f32[3,512,1536]{2,1,0:T(8,128)S(1)} fusion(bf16[512,3,128]{2,0,1:T(8,128)(2,1)S(1)} %bitcast.32, bf16[512,3,128]{2,0,1:T(8,128)(2,1)S(1)} %collective-permute-done.3, bf16[512,3,128]{2,0,1:T(8,128)(2,1)S(1)} %collective-permute-done.2, bf16[512,3,3,128]{0,3,2,1:T(8,128)(2,1)} %bitcast.29), kind=kOutput, calls=%fused_computation.28 | convolution fusion | flops 607518720 | bytes 11010048 | tf_op jit(solution)/shard_map/ihd,jhd->hij/dot_general | solution.py:64
  111.4 9.4 %fusion.39 = (f32[3,512]{1,0:T(4,128)S(1)}, f32[3,512,1536]{2,1,0:T(8,128)}) fusion(f32[3,512,1536]{2,1,0:T(8,128)S(1)} %fusion.21, pred[512,1536]{1,0:T(8,128)(4,1)} %and_and_fusion), kind=kOutput, calls=%fused_computation.63 | output fusion | flops 14157311 | bytes 19666944 | tf_op jit(solution)/shard_map/sub | solution.py:76
  120.8 3.9 %collective-permute-done.1 = bf16[512,3,128]{0,2,1:T(8,128)(2,1)} collective-permute-done((bf16[512,3,128]{0,2,1:T(8,128)(2,1)}, bf16[512,3,128]{0,2,1:T(8,128)(2,1)}, u32[]{:S(2)}, u32[]{:S(2)}) %collective-permute-start.1) | collective-permute-done | bytes 393248 | tf_op jit(solution)/shard_map/ppermute | solution.py:14
  124.8 5.8 %fusion.15 = f32[3,128,512]{2,1,0:T(8,128)S(1)} fusion(f32[3,512,1536]{2,1,0:T(8,128)} %get-tuple-element.7, f32[3,512]{1,0:T(4,128)S(1)} %get-tuple-element.6, bf16[512,3,128]{0,2,1:T(8,128)(2,1)} %get-tuple-element.4, bf16[512,3,128]{0,2,1:T(8,128)(2,1)} %collective-permute-done.1, bf16[512,3,128]{0,2,1:T(8,128)(2,1)} %collective-permute-done), kind=kOutput, calls=%fused_computation.22 | convolution fusion | flops 612630528 | bytes 11409408 | tf_op jit(solution)/shard_map/hij,jhd->ihd/dot_general | solution.py:78
  130.6 0.3 copy.35
  130.9 1.2 add_convert_fusion
  132.1 0.9 gather_fusion
  133.0 1.0 convolution_convert_fusion.1
  133.9 20.8 %all-to-all-start = ((bf16[4,64,384]{2,1,0:T(8,128)(2,1)}), bf16[4,64,384]{2,1,0:T(8,128)(2,1)S(1)}, u32[]{:S(2)}, u32[]{:S(2)}) async-start(bf16[4,64,384]{2,1,0:T(8,128)(2,1)} %bitcast.8), calls=%async_computation | async-start | bytes 393216 | tf_op jit(solution)/shard_map/all_to_all | solution.py:100
  154.8 3.0 %copy.37 = bf16[384,3072]{0,1:T(8,128)(2,1)S(1)} copy(bf16[384,3072]{1,0:T(8,128)(2,1)} %param.10) | data formatting | bytes 4718592 | tf_op args[3]
  157.8 2.6 %copy.38 = bf16[384,4,768]{2,0,1:T(8,128)(2,1)} copy(bf16[384,4,768]{0,2,1:T(8,128)(2,1)S(1)} %bitcast.27) | data formatting | bytes 4718592 | tf_op jit(solution)/shard_map/all_to_all | solution.py:20
  160.4 1.7 all-to-all-done
  162.1 3.6 %all-to-all-start.1 = ((bf16[384,4,768]{2,0,1:T(8,128)(2,1)}), bf16[384,4,768]{2,0,1:T(8,128)(2,1)S(1)}, u32[]{:S(2)}, u32[]{:S(2)}) async-start(bf16[384,4,768]{2,0,1:T(8,128)(2,1)} %copy.38), calls=%async_computation.1 | async-start | bytes 4718592 | tf_op jit(solution)/shard_map/all_to_all | solution.py:20
  165.7 35.5 %all_gather.7 = bf16[256,1536]{1,0:T(8,128)(2,1)S(1)} all-gather(bf16[256,384]{1,0:T(8,128)(2,1)S(1)} %bitcast.35), channel_id=1, replica_groups=mesh['seq'=4,'phase'=4,'dp'=2] {'phase'}, dimensions={1}, use_global_device_ids=true | all-gather | bytes 983040 | tf_op jit(solution)/shard_map/all_gather | solution.py:19
  201.2 1.2 copy.36
  202.4 2.2 %convert_reduce_fusion = f32[256,768]{1,0:T(8,128)S(1)} fusion(bf16[256,4,384]{0,2,1:T(8,128)(2,1)} %bitcast.33, bf16[384,4,768]{2,0,1:T(8,128)(2,1)S(1)} %all-to-all-done.1), kind=kOutput, calls=%fused_computation.10 | convolution fusion | flops 606142464 | bytes 3932160 | tf_op jit(solution)/shard_map/nsg,sgc->snc/dot_general | solution.py:24
  204.7 8.2 %psum.7 = f32[256]{0:T(256)S(1)} all-reduce(f32[256]{0:T(256)S(1)} %multiply_reduce_fusion.1), channel_id=1, replica_groups=mesh['seq'=4,'phase'=4,'dp'=2] {'phase'}, use_global_device_ids=true, to_apply=%region_6.7 | all-reduce | flops 256 | bytes 2048 | tf_op jit(solution)/shard_map/psum | solution.py:31
  212.9 0.9 multiply_convert_fusion.2
  (29 shorter events, 0.7 us)
Async XLA Ops:
  7.2 2.5 %copy-start = (bf16[512,1536]{1,0:T(8,128)(2,1)S(1)}, bf16[512,1536]{1,0:T(8,128)(2,1)}, u32[]{:S(2)}) copy-start(bf16[512,1536]{1,0:T(8,128)(2,1)} %param.7) | copy-start | bytes 4718596
  7.2 75.0 %all-gather.2.cloned.1.call-start = ((), (), s32[]{:S(2)}) async-start(), calls=%async_computation.2 | async-start | bytes 4423680 | tf_op jit(solution)/shard_map/all_gather | solution.py:47
  9.6 2.1 copy-start.4
  9.6 2.1 copy-start.6
  9.7 72.5 %copy-start.5 = (f32[1536]{0:T(1024)S(1)}, f32[1536]{0:T(1024)}, u32[]{:S(2)}) copy-start(f32[1536]{0:T(1024)} %param.8) | copy-start | bytes 18436
  87.1 13.5 %copy-start.1 = (bf16[512,1152]{0,1:T(8,128)(2,1)}, bf16[512,1152]{0,1:T(8,128)(2,1)S(1)}, u32[]{:S(2)}) copy-start(bf16[512,1152]{0,1:T(8,128)(2,1)S(1)} %copy.32) | copy-start | bytes 3538948
  88.2 12.4 %collective-permute-start.2 = (bf16[512,3,128]{2,0,1:T(8,128)(2,1)S(1)}, bf16[512,3,128]{2,0,1:T(8,128)(2,1)S(1)}, u32[]{:S(2)}, u32[]{:S(2)}) collective-permute-start(bf16[512,3,128]{2,0,1:T(8,128)(2,1)S(1)} %bitcast.30), channel_id=1, source_target_pairs={{0,16},{8,24},{1,17},{9,25},{2,18},{10,26},{3,19},{11,27},{4,20},{... | collective-permute-start | bytes 1179656 | tf_op jit(solution)/shard_map/ppermute | solution.py:14
  91.1 17.9 %collective-permute-start.3 = (bf16[512,3,128]{2,0,1:T(8,128)(2,1)S(1)}, bf16[512,3,128]{2,0,1:T(8,128)(2,1)S(1)}, u32[]{:S(2)}, u32[]{:S(2)}) collective-permute-start(bf16[512,3,128]{2,0,1:T(8,128)(2,1)S(1)} %bitcast.31), channel_id=1, source_target_pairs={{0,8},{8,16},{16,24},{1,9},{9,17},{17,25},{2,10},{10,18},{18,26},{... | collective-permute-start | bytes 1179656 | tf_op jit(solution)/shard_map/ppermute | solution.py:14
  95.3 25.6 %collective-permute-start = (bf16[512,3,128]{0,2,1:T(8,128)(2,1)}, bf16[512,3,128]{0,2,1:T(8,128)(2,1)}, u32[]{:S(2)}, u32[]{:S(2)}) collective-permute-start(bf16[512,3,128]{0,2,1:T(8,128)(2,1)} %get-tuple-element.4), channel_id=1, source_target_pairs={{0,16},{8,24},{1,17},{9,25},{2,18},{10,26},{3,19},{11,27},{4,20},{... | collective-permute-start | bytes 1179656 | tf_op jit(solution)/shard_map/ppermute | solution.py:14
  97.3 27.5 %collective-permute-start.1 = (bf16[512,3,128]{0,2,1:T(8,128)(2,1)}, bf16[512,3,128]{0,2,1:T(8,128)(2,1)}, u32[]{:S(2)}, u32[]{:S(2)}) collective-permute-start(bf16[512,3,128]{0,2,1:T(8,128)(2,1)} %get-tuple-element.4), channel_id=1, source_target_pairs={{0,8},{8,16},{16,24},{1,9},{9,17},{17,25},{2,10},{10,18},{18,26},{... | collective-permute-start | bytes 1179656 | tf_op jit(solution)/shard_map/ppermute | solution.py:14
  132.1 25.7 %copy-start.2 = (bf16[512,384]{1,0:T(8,128)(2,1)}, bf16[512,384]{1,0:T(8,128)(2,1)S(1)}, u32[]{:S(2)}) copy-start(bf16[512,384]{1,0:T(8,128)(2,1)S(1)} %add_convert_fusion) | copy-start | bytes 1179652
  133.9 28.1 %all-to-all-start = ((bf16[4,64,384]{2,1,0:T(8,128)(2,1)}), bf16[4,64,384]{2,1,0:T(8,128)(2,1)S(1)}, u32[]{:S(2)}, u32[]{:S(2)}) async-start(bf16[4,64,384]{2,1,0:T(8,128)(2,1)} %bitcast.8), calls=%async_computation | async-start | bytes 393216 | tf_op jit(solution)/shard_map/all_to_all | solution.py:100
  162.1 40.3 %all-to-all-start.1 = ((bf16[384,4,768]{2,0,1:T(8,128)(2,1)}), bf16[384,4,768]{2,0,1:T(8,128)(2,1)S(1)}, u32[]{:S(2)}, u32[]{:S(2)}) async-start(bf16[384,4,768]{2,0,1:T(8,128)(2,1)} %copy.38), calls=%async_computation.1 | async-start | bytes 4718592 | tf_op jit(solution)/shard_map/all_to_all | solution.py:20
  202.4 10.6 %copy-start.3 = (f32[768]{0:T(1024)S(1)}, f32[768]{0:T(1024)}, u32[]{:S(2)}) copy-start(f32[768]{0:T(1024)} %param.11) | copy-start | bytes 9220
Sparse Core Ops, SparseCore 0:
  9.7 72.4 all-gather.1
where the time goes:
time: 221 us
  waiting for transfers between devices  84.5 us (38%)
  blocking collectives  43.7 us (20%)
  starting transfers between devices  34.5 us (16%)
  other arithmetic  16 us (7%)
  matrix products  15.7 us (7%)
  between operations  14.3 us (6%)
  local copies, waits for them, and re-layouts  12 us (5%)
    all_gather x1, waiting for transfers between devices, on_device(): piece = lax.all_gather(w_qkv, 'seq', axis=0, tiled=True)  69.8 us
    all_gather x1, blocking collectives, project_rows(): full_rows = lax.all_gather(rows, 'phase', axis=1, tiled=True)  35.5 us
    all_to_all x1, starting transfers between devices, on_device(): lax.all_to_all(outgoing, 'seq', split_axis=0, concat_axis=0, tiled=True)  20.8 us
    ppermute x4, waiting for transfers between devices, passed_along(): return lax.ppermute(value, axis, pairs)  13 us
    ppermute x4, starting transfers between devices, passed_along(): return lax.ppermute(value, axis, pairs)  10 us
    sub x1, other arithmetic, on_device(): expo = jnp.exp(scores - top)  9.4 us
    psum x1, blocking collectives, project_rows(): squares = lax.psum(jnp.sum(projected * projected, axis=1), 'phase')  8.2 us
    dot_general x1, matrix products, on_device(): jnp.einsum('hij,jhd->ihd', probs, value_all, preferred_element_type=jnp.f...  5.83 us
  transfers between devices with their start and end apart: 7, of which 5 were waited for; matrix products, arithmetic and copies ran while one was open for 10% of the time, Pallas kernels for 0%

commit v1 on v0

--- a/solution.py
+++ b/solution.py
@@ -6,6 +6,18 @@
 DC = 3072
 HD = 128
 WINDOW = 1024
+
+
+def sent_to_each(x, axis, split, join):
+    ways, here = (lax.axis_size(axis), lax.axis_index(axis))
+    width = x.shape[split] // ways
+    turned = jnp.roll(x, -here * width, axis=split)
+    got = [lax.slice_in_dim(turned, 0, width, axis=split)]
+    for far in range(1, ways):
+        sent = lax.slice_in_dim(turned, far * width, (far + 1) * width, axis=split)
+        got.append(lax.ppermute(sent, axis, [(d, (d + far) % ways) for d in range(ways)]))
+    line = jnp.concatenate(got[::-1], axis=join)
+    return jnp.roll(line, (here + 1) * got[0].shape[join], axis=join)
 
 
 def passed_along(value, axis, by):
@@ -97,9 +109,7 @@
         jnp.bfloat16
     )
     outgoing = outgoing.reshape(n_seq, slot_count, width_dev)
-    arrived = lax.all_to_all(outgoing, "seq", split_axis=0, concat_axis=0, tiled=True).reshape(
-        n_seq * slot_count, width_dev
-    )
+    arrived = sent_to_each(outgoing, "seq", 0, 0).reshape(n_seq * slot_count, width_dev)
     stretch_states = project_rows(arrived, w_up, out_gain)
     return (byte_states, stretch_states)
 

time: 221 us -> 193 us (0.87)
  blocking collectives: 43.7 us -> 22.3 us
  waiting for transfers between devices: 84.5 us -> 76.3 us
  starting transfers between devices: 34.5 us -> 36.9 us
    all_gather x1, blocking collectives: 35.5 us -> 13.4 us  [project_rows(): full_rows = lax.all_gather(rows, 'phase', axis=1, tiled=True)]
    ppermute x0 -> x3, starting transfers between devices: none -> 22.1 us  [sent_to_each(): lax.ppermute(sent, axis, [(d, (d + far) % ways) for d in range(ways)])]
    all_to_all x1 -> x0, starting transfers between devices: 20.8 us -> none  [on_device(): lax.all_to_all(outgoing, 'seq', split_axis=0, concat_axis=0, tiled=True)]
    all_gather x1, waiting for transfers between devices: 69.8 us -> 58.9 us  [on_device(): piece = lax.all_gather(w_qkv, 'seq', axis=0, tiled=True)]
    ppermute x0 -> x3, waiting for transfers between devices: none -> 5.25 us  [sent_to_each(): lax.ppermute(sent, axis, [(d, (d + far) % ways) for d in range(ways)])]
  transfers between devices with their start and end apart: 7 -> 9, of which waited for: 5 -> 6; matrix products, arithmetic and copies ran while one was open for 10% -> 19% of each run, Pallas kernels for 0% -> 0%
where the time goes in v1:
time: 193 us
  waiting for transfers between devices  76.3 us (40%)
  starting transfers between devices  36.9 us (19%)
  blocking collectives  22.3 us (12%)
  other arithmetic  16.4 us (8%)
  matrix products  15.5 us (8%)
  between operations  14.3 us (7%)
  local copies, waits for them, and re-layouts  11.1 us (6%)
    all_gather x1, waiting for transfers between devices, on_device(): piece = lax.all_gather(w_qkv, 'seq', axis=0, tiled=True)  58.9 us
    ppermute x3, starting transfers between devices, sent_to_each(): lax.ppermute(sent, axis, [(d, (d + far) % ways) for d in range(ways)])  22.1 us
    all_gather x1, blocking collectives, project_rows(): full_rows = lax.all_gather(rows, 'phase', axis=1, tiled=True)  13.4 us
    ppermute x4, waiting for transfers between devices, passed_along(): return lax.ppermute(value, axis, pairs)  12.2 us
    sub x1, other arithmetic, on_device(): expo = jnp.exp(scores - top)  9.51 us
    ppermute x4, starting transfers between devices, passed_along(): return lax.ppermute(value, axis, pairs)  9.44 us
    psum x1, blocking collectives, project_rows(): squares = lax.psum(jnp.sum(projected * projected, axis=1), 'phase')  8.91 us
    dot_general x1, matrix products, on_device(): jnp.einsum('hij,jhd->ihd', probs, value_all, preferred_element_type=jnp.f...  5.83 us
  transfers between devices with their start and end apart: 9, of which 6 were waited for; matrix products, arithmetic and copies ran while one was open for 19% of the time, Pallas kernels for 0%

profile of v1, /device:TPU:0, one launch (start us, length us, event | category | flops | bytes accessed | tf_op | source)
XLA Modules:
  0.0 192.9 jit_solution(7715281674371067789)
XLA Ops:
  7.2 2.3 %copy.31 = bf16[384,3,384]{0,2,1:T(8,128)(2,1)} copy(bf16[384,3,384]{2,0,1:T(8,128)(2,1)} %param.11) | data formatting | bytes 1769472 | tf_op args[2]
  9.5 3.0 %copy.37 = bf16[384,3072]{0,1:T(8,128)(2,1)S(1)} copy(bf16[384,3072]{1,0:T(8,128)(2,1)} %param.12) | data formatting | bytes 4718592 | tf_op args[3]
  12.5 2.6 %copy.38 = bf16[384,4,768]{2,0,1:T(8,128)(2,1)} copy(bf16[384,4,768]{0,2,1:T(8,128)(2,1)S(1)} %bitcast.27) | data formatting | bytes 4718592 | tf_op jit(solution)/shard_map/all_to_all | solution.py:32
  15.1 5.3 %all-to-all-start = ((bf16[384,4,768]{2,0,1:T(8,128)(2,1)}), bf16[384,4,768]{2,0,1:T(8,128)(2,1)}, u32[]{:S(2)}, u32[]{:S(2)}) async-start(bf16[384,4,768]{2,0,1:T(8,128)(2,1)} %copy.38), calls=%async_computation | async-start | bytes 4718592 | tf_op jit(solution)/shard_map/all_to_all | solution.py:32
  20.5 2.0 %convert_element_type.44 = f32[512,1536]{1,0:T(8,128)} convert(bf16[512,1536]{1,0:T(8,128)(2,1)S(1)} %copy-done) | non-fusion elementwise | flops 786432 | bytes 4718592 | tf_op jit(solution)/shard_map/convert_element_type | solution.py:55
  22.8 0.4 multiply_reduce_fusion
  23.2 58.9 %all-gather.2.cloned.1.call-done = bf16[1536,3,384]{0,2,1:T(8,128)(2,1)} async-done(((bf16[384,3,384]{0,2,1:T(8,128)(2,1)}), bf16[1536,3,384]{0,2,1:T(8,128)(2,1)}) %all-gather.2.cloned.1.call-update) | async-done | bytes 3538960 | tf_op jit(solution)/shard_map/all_gather | solution.py:59
  82.1 4.2 %convolution_convert_fusion = bf16[512,1152]{1,0:T(8,128)(2,1)S(1)} fusion(bf16[1536,1152]{0,1:T(8,128)(2,1)} %bitcast.37, f32[1536]{0:T(1024)S(1)} %copy-done.5, f32[512]{0:T(512)S(1)} %add_rsqrt_fusion, bf16[512,1536]{1,0:T(8,128)(2,1)S(1)} %copy-done), kind=kOutput, calls=%fused_computation.14 | convolution fusion | flops 1815674880 | bytes 6299648 | tf_op jit(solution)/shard_map/dot_general | solution.py:60
  86.4 0.6 copy.32
  87.0 0.9 slice_bitcast_fusion.2
  88.1 1.7 collective-permute-start.3
  89.8 3.6 %collective-permute-start.2 = (bf16[512,3,128]{2,0,1:T(8,128)(2,1)S(1)}, bf16[512,3,128]{2,0,1:T(8,128)(2,1)S(1)}, u32[]{:S(2)}, u32[]{:S(2)}) collective-permute-start(bf16[512,3,128]{2,0,1:T(8,128)(2,1)S(1)} %bitcast.31), channel_id=1, source_target_pairs={{0,16},{8,24},{1,17},{9,25},{2,18},{10,26},{3,19},{11,27},{4,20},{... | collective-permute-start | bytes 1179656 | tf_op jit(solution)/shard_map/ppermute | solution.py:26
  93.5 1.7 and_and_fusion
  95.2 2.1 %collective-permute-start.1 = (bf16[512,3,128]{0,2,1:T(8,128)(2,1)}, bf16[512,3,128]{0,2,1:T(8,128)(2,1)}, u32[]{:S(2)}, u32[]{:S(2)}) collective-permute-start(bf16[512,3,128]{0,2,1:T(8,128)(2,1)} %get-tuple-element.5), channel_id=1, source_target_pairs={{0,8},{8,16},{16,24},{1,9},{9,17},{17,25},{2,10},{10,18},{18,26},{... | collective-permute-start | bytes 1179656 | tf_op jit(solution)/shard_map/ppermute | solution.py:26
  97.3 2.0 %collective-permute-start = (bf16[512,3,128]{0,2,1:T(8,128)(2,1)}, bf16[512,3,128]{0,2,1:T(8,128)(2,1)}, u32[]{:S(2)}, u32[]{:S(2)}) collective-permute-start(bf16[512,3,128]{0,2,1:T(8,128)(2,1)} %get-tuple-element.5), channel_id=1, source_target_pairs={{0,16},{8,24},{1,17},{9,25},{2,18},{10,26},{3,19},{11,27},{4,20},{... | collective-permute-start | bytes 1179656 | tf_op jit(solution)/shard_map/ppermute | solution.py:26
  99.3 8.5 %collective-permute-done.2 = bf16[512,3,128]{2,0,1:T(8,128)(2,1)S(1)} collective-permute-done((bf16[512,3,128]{2,0,1:T(8,128)(2,1)S(1)}, bf16[512,3,128]{2,0,1:T(8,128)(2,1)S(1)}, u32[]{:S(2)}, u32[]{:S(2)}) %collective-permute-start.2) | collective-permute-done | bytes 393248 | tf_op jit(solution)/shard_map/ppermute | solution.py:26
  107.8 2.4 %fusion.21 = f32[3,512,1536]{2,1,0:T(8,128)S(1)} fusion(bf16[512,3,128]{2,0,1:T(8,128)(2,1)S(1)} %bitcast.32, bf16[512,3,128]{2,0,1:T(8,128)(2,1)S(1)} %collective-permute-done.3, bf16[512,3,128]{2,0,1:T(8,128)(2,1)S(1)} %collective-permute-done.2, bf16[512,3,3,128]{0,3,2,1:T(8,128)(2,1)} %bitcast.29), kind=kOutput, calls=%fused_computation.28 | convolution fusion | flops 607518720 | bytes 11010048 | tf_op jit(solution)/shard_map/ihd,jhd->hij/dot_general | solution.py:76
  110.2 9.5 %fusion.48 = (f32[3,512]{1,0:T(4,128)S(1)}, f32[3,512,1536]{2,1,0:T(8,128)}) fusion(f32[3,512,1536]{2,1,0:T(8,128)S(1)} %fusion.21, pred[512,1536]{1,0:T(8,128)(4,1)} %and_and_fusion), kind=kOutput, calls=%fused_computation.82 | output fusion | flops 14157311 | bytes 19666944 | tf_op jit(solution)/shard_map/sub | solution.py:88
  119.7 3.7 %collective-permute-done = bf16[512,3,128]{0,2,1:T(8,128)(2,1)} collective-permute-done((bf16[512,3,128]{0,2,1:T(8,128)(2,1)}, bf16[512,3,128]{0,2,1:T(8,128)(2,1)}, u32[]{:S(2)}, u32[]{:S(2)}) %collective-permute-start) | collective-permute-done | bytes 393248 | tf_op jit(solution)/shard_map/ppermute | solution.py:26
  123.4 5.8 %fusion.15 = f32[3,128,512]{2,1,0:T(8,128)S(1)} fusion(f32[3,512,1536]{2,1,0:T(8,128)} %get-tuple-element.12, f32[3,512]{1,0:T(4,128)S(1)} %get-tuple-element.11, bf16[512,3,128]{0,2,1:T(8,128)(2,1)} %get-tuple-element.5, bf16[512,3,128]{0,2,1:T(8,128)(2,1)} %collective-permute-done.1, bf16[512,3,128]{0,2,1:T(8,128)(2,1)} %collective-permute-done), kind=kOutput, calls=%fused_computation.22 | convolution fusion | flops 612630528 | bytes 11409408 | tf_op jit(solution)/shard_map/hij,jhd->ihd/dot_general | solution.py:90
  129.5 1.2 add_convert_fusion
  130.7 0.9 gather_fusion
  131.6 0.3 convolution_convert_fusion.1
  132.0 21.5 %collective-permute-start.4 = (bf16[1,64,384]{2,1,0:T(8,128)(2,1)S(1)}, bf16[1,64,384]{2,1,0:T(8,128)(2,1)S(1)}, u32[]{:S(2)}, u32[]{:S(2)}) collective-permute-start(bf16[1,64,384]{2,1,0:T(8,128)(2,1)S(1)} %get-tuple-element.10), channel_id=1, source_target_pairs={{0,24},{8,0},{16,8},{24,16},{1,25},{9,1},{17,9},{25,17},{2,26},{10... | collective-permute-start | bytes 147464 | tf_op jit(solution)/shard_map/ppermute | solution.py:18
  153.5 0.6 collective-permute-start.6
  154.2 1.1 collective-permute-done.4
  155.3 3.2 %collective-permute-done.5 = bf16[1,64,384]{2,1,0:T(8,128)(2,1)S(1)} collective-permute-done((bf16[1,64,384]{2,1,0:T(8,128)(2,1)S(1)}, bf16[1,64,384]{2,1,0:T(8,128)(2,1)S(1)}, u32[]{:S(2)}, u32[]{:S(2)}) %collective-permute-start.5) | collective-permute-done | bytes 49184 | tf_op jit(solution)/shard_map/ppermute | solution.py:18
  158.5 0.9 collective-permute-done.6
  159.6 13.4 %all_gather.7 = bf16[256,1536]{1,0:T(8,128)(2,1)S(1)} all-gather(bf16[256,384]{1,0:T(8,128)(2,1)S(1)} %bitcast.36), channel_id=1, replica_groups=mesh['seq'=4,'phase'=4,'dp'=2] {'phase'}, dimensions={1}, use_global_device_ids=true | all-gather | bytes 983040 | tf_op jit(solution)/shard_map/all_gather | solution.py:31
  173.3 2.8 %convert_reduce_fusion = f32[256,768]{1,0:T(8,128)S(1)} fusion(bf16[256,4,384]{0,2,1:T(8,128)(2,1)S(1)} %bitcast.33, bf16[384,4,768]{2,0,1:T(8,128)(2,1)} %all-to-all-done), kind=kOutput, calls=%fused_computation.10 | convolution fusion | flops 606142464 | bytes 3932160 | tf_op jit(solution)/shard_map/nsg,sgc->snc/dot_general | solution.py:36
  176.2 8.9 %psum.7 = f32[256]{0:T(256)S(1)} all-reduce(f32[256]{0:T(256)S(1)} %multiply_reduce_fusion.1), channel_id=1, replica_groups=mesh['seq'=4,'phase'=4,'dp'=2] {'phase'}, use_global_device_ids=true, to_apply=%region_6.8 | all-reduce | flops 256 | bytes 2048 | tf_op jit(solution)/shard_map/psum | solution.py:43
  185.1 0.9 multiply_convert_fusion.2
  (36 shorter events, 1.6 us)
Async XLA Ops:
  7.2 74.9 %all-gather.2.cloned.1.call-start = ((), (), s32[]{:S(2)}) async-start(), calls=%async_computation.1 | async-start | bytes 4423680 | tf_op jit(solution)/shard_map/all_gather | solution.py:59
  15.1 5.3 %copy-start = (bf16[512,1536]{1,0:T(8,128)(2,1)S(1)}, bf16[512,1536]{1,0:T(8,128)(2,1)}, u32[]{:S(2)}) copy-start(bf16[512,1536]{1,0:T(8,128)(2,1)} %param.9) | copy-start | bytes 4718596
  15.1 158.1 %all-to-all-start = ((bf16[384,4,768]{2,0,1:T(8,128)(2,1)}), bf16[384,4,768]{2,0,1:T(8,128)(2,1)}, u32[]{:S(2)}, u32[]{:S(2)}) async-start(bf16[384,4,768]{2,0,1:T(8,128)(2,1)} %copy.38), calls=%async_computation | async-start | bytes 4718592 | tf_op jit(solution)/shard_map/all_to_all | solution.py:32
  20.5 2.1 %copy-start.4 = (s32[128]{0:T(128)S(1)}, s32[128]{0:T(128)}, u32[]{:S(2)}) copy-start(s32[128]{0:T(128)} %param.14) | copy-start | bytes 1540
  20.5 2.1 %copy-start.6 = (s32[128,1]{0,1:T(1,128)S(1)}, s32[128,1]{0,1:T(1,128)}, u32[]{:S(2)}) copy-start(s32[128,1]{0,1:T(1,128)} %param.15) | copy-start | bytes 1540
  20.5 61.6 %copy-start.5 = (f32[1536]{0:T(1024)S(1)}, f32[1536]{0:T(1024)}, u32[]{:S(2)}) copy-start(f32[1536]{0:T(1024)} %param.10) | copy-start | bytes 18436
  87.0 12.3 %copy-start.1 = (bf16[512,1152]{0,1:T(8,128)(2,1)}, bf16[512,1152]{0,1:T(8,128)(2,1)S(1)}, u32[]{:S(2)}) copy-start(bf16[512,1152]{0,1:T(8,128)(2,1)S(1)} %copy.32) | copy-start | bytes 3538948
  88.1 11.1 %collective-permute-start.3 = (bf16[512,3,128]{2,0,1:T(8,128)(2,1)S(1)}, bf16[512,3,128]{2,0,1:T(8,128)(2,1)S(1)}, u32[]{:S(2)}, u32[]{:S(2)}) collective-permute-start(bf16[512,3,128]{2,0,1:T(8,128)(2,1)S(1)} %bitcast.30), channel_id=1, source_target_pairs={{0,8},{8,16},{16,24},{1,9},{9,17},{17,25},{2,10},{10,18},{18,26},{... | collective-permute-start | bytes 1179656 | tf_op jit(solution)/shard_map/ppermute | solution.py:26
  89.8 17.9 %collective-permute-start.2 = (bf16[512,3,128]{2,0,1:T(8,128)(2,1)S(1)}, bf16[512,3,128]{2,0,1:T(8,128)(2,1)S(1)}, u32[]{:S(2)}, u32[]{:S(2)}) collective-permute-start(bf16[512,3,128]{2,0,1:T(8,128)(2,1)S(1)} %bitcast.31), channel_id=1, source_target_pairs={{0,16},{8,24},{1,17},{9,25},{2,18},{10,26},{3,19},{11,27},{4,20},{... | collective-permute-start | bytes 1179656 | tf_op jit(solution)/shard_map/ppermute | solution.py:26
  95.2 24.5 %collective-permute-start.1 = (bf16[512,3,128]{0,2,1:T(8,128)(2,1)}, bf16[512,3,128]{0,2,1:T(8,128)(2,1)}, u32[]{:S(2)}, u32[]{:S(2)}) collective-permute-start(bf16[512,3,128]{0,2,1:T(8,128)(2,1)} %get-tuple-element.5), channel_id=1, source_target_pairs={{0,8},{8,16},{16,24},{1,9},{9,17},{17,25},{2,10},{10,18},{18,26},{... | collective-permute-start | bytes 1179656 | tf_op jit(solution)/shard_map/ppermute | solution.py:26
  97.3 26.2 %collective-permute-start = (bf16[512,3,128]{0,2,1:T(8,128)(2,1)}, bf16[512,3,128]{0,2,1:T(8,128)(2,1)}, u32[]{:S(2)}, u32[]{:S(2)}) collective-permute-start(bf16[512,3,128]{0,2,1:T(8,128)(2,1)} %get-tuple-element.5), channel_id=1, source_target_pairs={{0,16},{8,24},{1,17},{9,25},{2,18},{10,26},{3,19},{11,27},{4,20},{... | collective-permute-start | bytes 1179656 | tf_op jit(solution)/shard_map/ppermute | solution.py:26
  130.7 42.5 %copy-start.2 = (bf16[512,384]{1,0:T(8,128)(2,1)}, bf16[512,384]{1,0:T(8,128)(2,1)S(1)}, u32[]{:S(2)}) copy-start(bf16[512,384]{1,0:T(8,128)(2,1)S(1)} %add_convert_fusion) | copy-start | bytes 1179652
  132.0 23.2 %collective-permute-start.4 = (bf16[1,64,384]{2,1,0:T(8,128)(2,1)S(1)}, bf16[1,64,384]{2,1,0:T(8,128)(2,1)S(1)}, u32[]{:S(2)}, u32[]{:S(2)}) collective-permute-start(bf16[1,64,384]{2,1,0:T(8,128)(2,1)S(1)} %get-tuple-element.10), channel_id=1, source_target_pairs={{0,24},{8,0},{16,8},{24,16},{1,25},{9,1},{17,9},{25,17},{2,26},{10... | collective-permute-start | bytes 147464 | tf_op jit(solution)/shard_map/ppermute | solution.py:18
  153.5 5.0 %collective-permute-start.5 = (bf16[1,64,384]{2,1,0:T(8,128)(2,1)S(1)}, bf16[1,64,384]{2,1,0:T(8,128)(2,1)S(1)}, u32[]{:S(2)}, u32[]{:S(2)}) collective-permute-start(bf16[1,64,384]{2,1,0:T(8,128)(2,1)S(1)} %get-tuple-element.9), channel_id=1, source_target_pairs={{0,16},{8,24},{16,0},{24,8},{1,17},{9,25},{17,1},{25,9},{2,18},{10... | collective-permute-start | bytes 147464 | tf_op jit(solution)/shard_map/ppermute | solution.py:18
  153.5 5.9 %collective-permute-start.6 = (bf16[1,64,384]{2,1,0:T(8,128)(2,1)S(1)}, bf16[1,64,384]{2,1,0:T(8,128)(2,1)S(1)}, u32[]{:S(2)}, u32[]{:S(2)}) collective-permute-start(bf16[1,64,384]{2,1,0:T(8,128)(2,1)S(1)} %get-tuple-element.8), channel_id=1, source_target_pairs={{0,8},{8,16},{16,24},{24,0},{1,9},{9,17},{17,25},{25,1},{2,10},{10... | collective-permute-start | bytes 147464 | tf_op jit(solution)/shard_map/ppermute | solution.py:18
  173.3 11.8 %copy-start.3 = (f32[768]{0:T(1024)S(1)}, f32[768]{0:T(1024)}, u32[]{:S(2)}) copy-start(f32[768]{0:T(1024)} %param.13) | copy-start | bytes 9220
Sparse Core Ops, SparseCore 0:
  9.6 72.4 all-gather.1
